TPU v7x, 32 devices: a whole 2x2x4 slice. The times are simulated.
32 devices in a mesh: row: 8 (over y, x, core), col: 4 (over z).
Axes of the slice: x: 2, y: 2, z: 4, core: 2. Of those that a mesh axis runs over, the one named last changes fastest.
Arguments:
- tokens: bfloat16 [128, 96, 768], P('row', 'col'), as said below
- dw_kernel: float32 [7, 7, 768], replicated, may hold values from -0.875 to 0.875
- norm_gain: float32 [768], replicated, may hold values from 0.5 to 1.5
- norm_shift: float32 [768], replicated, may hold values from -3 to 3
- w_in: bfloat16 [768, 3072], P(None, 'col'), may hold values from -0.21875 to 0.21875
- w_out: bfloat16 [3072, 768], P('col'), may hold values from -0.109375 to 0.109375
- w_kv: bfloat16 [768, 1536], P(None, 'col'), as said below
- queries: bfloat16 [512, 768], replicated, may hold values from -300 to 300, as said below
- latent_gain: float32 [768], replicated, may hold values from 0.5 to 1.5
- w_o: bfloat16 [768, 768], P(None, 'col'), may hold values from -0.21875 to 0.21875
Outputs:
- token_map: bfloat16 [128, 96, 768], P('row', 'col')
- latents: bfloat16 [512, 768], replicated
Inputs may be any that keep to these rules, and one draw needn't show every extreme that they name: Latent queries; a few rows may be far larger than the others. `tokens`: patch token features, roughly unit normal, between -24 and 24; a few cells hold 24 in two channels. `w_kv`: key and value projection weights.
All inputs are finite; a program needn't handle non-finite values.
Results may differ from a plain program's by a relative error of at most 0.011.
Values may be sent and summed in bfloat16 or wider, within the bound.
A program may use at most 64 MiB of HBM per device.

v0:
```python
import math
import jax
import jax.numpy as jnp
from jax import lax
from jax.sharding import PartitionSpec as P

HEADS = 12
HEAD = 64


def with_halo(cells, sides, width):
    for axis, dim in sides:
        count = lax.axis_size(axis)
        ends = count - 1
        head = lax.slice_in_dim(cells, 0, width, axis=dim)
        tail = lax.slice_in_dim(cells, cells.shape[dim] - width, cells.shape[dim], axis=dim)
        cells = jnp.concatenate(
            [
                lax.ppermute(tail, axis, [(i, (i + 1) % count) for i in range(ends)]),
                cells,
                lax.ppermute(head, axis, [((i + 1) % count, i) for i in range(ends)]),
            ],
            axis=dim,
        )
    return cells


def conv_taps(padded, height, width, dw_kernel):
    mixed = jnp.zeros((height, width, padded.shape[2]), jnp.float32)
    for row_tap in range(7):
        for col_tap in range(7):
            mixed = (
                mixed
                + padded[row_tap : row_tap + height, col_tap : col_tap + width]
                * dw_kernel[row_tap, col_tap]
            )
    return mixed


def layer_norm(mixed, norm_gain, norm_shift):
    center = mixed - jnp.mean(mixed, axis=-1, keepdims=True)
    spread = jnp.mean(center * center, axis=-1, keepdims=True)
    return (center * lax.rsqrt(spread + 1e-06) * norm_gain + norm_shift).astype(jnp.bfloat16)


def finish_latents(numer, denom, latent_gain, w_full):
    attended = (numer / denom[..., None]).reshape(numer.shape[0], -1)
    squares = jnp.mean(attended * attended, axis=-1, keepdims=True)
    scaled = (attended * lax.rsqrt(squares + 1e-06) * latent_gain).astype(jnp.bfloat16)
    return jnp.dot(scaled, w_full, preferred_element_type=jnp.float32).astype(jnp.bfloat16)


def body(tokens, dw_kernel, norm_gain, norm_shift, w_in, w_out, w_kv, queries, latent_gain, w_o):
    height, width, width_d = tokens.shape
    latent_count = queries.shape[0]
    padded = with_halo(tokens, (("row", 0), ("col", 1)), 3)
    mixed = conv_taps(padded.astype(jnp.float32), height, width, dw_kernel)
    normed = layer_norm(mixed, norm_gain, norm_shift).reshape(height * width, width_d)
    residual = tokens.reshape(height * width, width_d).astype(jnp.float32)
    hidden = jax.nn.gelu(
        jnp.dot(
            normed,
            lax.all_gather(w_in, "col", axis=1, tiled=True),
            preferred_element_type=jnp.float32,
        )
    ).astype(jnp.bfloat16)
    update = jnp.dot(
        hidden, lax.all_gather(w_out, "col", axis=0, tiled=True), preferred_element_type=jnp.float32
    )
    token_rows = (residual + update).astype(jnp.bfloat16)
    token_map = token_rows.reshape(height, width, width_d)
    keys_vals = jnp.dot(
        token_rows,
        lax.all_gather(w_kv, "col", axis=1, tiled=True),
        preferred_element_type=jnp.float32,
    ).astype(jnp.bfloat16)
    w_full = lax.all_gather(w_o, "col", axis=1, tiled=True)
    key_heads = keys_vals[:, :width_d].reshape(-1, HEADS, HEAD)
    val_heads = keys_vals[:, width_d:].reshape(-1, HEADS, HEAD)
    query_heads = queries.reshape(latent_count, HEADS, HEAD)
    score_scale = 1.0 / math.sqrt(HEAD)
    group_size = math.gcd(HEADS, 4)
    max_parts, den_parts, num_parts = ([], [], [])
    for first_head in range(0, HEADS, group_size):
        scores = (
            jnp.einsum(
                "lhd,thd->lht",
                query_heads[:, first_head : first_head + group_size],
                key_heads[:, first_head : first_head + group_size],
                preferred_element_type=jnp.float32,
            )
            * score_scale
        )
        local_max = jnp.max(scores, axis=-1)
        weights = jnp.exp(scores - local_max[..., None])
        den_parts.append(jnp.sum(weights, axis=-1))
        max_parts.append(local_max)
        num_parts.append(
            jnp.einsum(
                "lht,thd->lhd",
                weights.astype(jnp.bfloat16),
                val_heads[:, first_head : first_head + group_size],
                preferred_element_type=jnp.float32,
            )
        )
    maxima = jnp.concatenate(max_parts, axis=1)
    denom = jnp.concatenate(den_parts, axis=1)
    numer = jnp.concatenate(num_parts, axis=1)
    peak = lax.pmax(maxima, ("row", "col"))
    factor = jnp.exp(maxima - peak)
    den_terms = denom * factor
    num_terms = (numer * factor[..., None]).reshape(latent_count, width_d)
    den_part, num_part = (
        lax.psum_scatter(den_terms, "col", scatter_dimension=0, tiled=True),
        lax.psum_scatter(num_terms, "col", scatter_dimension=0, tiled=True),
    )
    den_share, num_share = lax.psum((den_part, num_part), "row")
    own_rows = finish_latents(
        num_share.reshape(num_share.shape[0], HEADS, HEAD), den_share, latent_gain, w_full
    )
    latents = lax.all_gather(own_rows, "col", axis=0, tiled=True)
    return (token_map, latents)


def solution(mesh):
    in_specs = (
        P("row", "col", None),
        P(),
        P(),
        P(),
        P(None, "col"),
        P("col", None),
        P(None, "col"),
        P(),
        P(),
        P(None, "col"),
    )
    out_specs = (P("row", "col", None), P())
    return jax.shard_map(body, mesh=mesh, in_specs=in_specs, out_specs=out_specs, check_vma=False)
```

profile of v0, /device:TPU:0, one launch (start us, length us, event | category | flops | bytes accessed | tf_op | source)
XLA Modules:
  0.0 479.7 jit_solution(5248755326156885472)
XLA Ops:
  8.8 2.4 collective-permute-start
  14.1 2.3 collective-permute-done.1
  16.6 3.5 collective-permute-start.2
  21.5 4.3 collective-permute-done.2
  25.8 7.4 %collective-permute-done.3 = bf16[22,3,768]{2,1,0:T(4,128)(2,1)S(1)} collective-permute-done((bf16[22,3,768]{2,1,0:T(4,128)(2,1)S(1)}, bf16[22,3,768]{2,1,0:T(4,128)(2,1)S(1)}, u32[]{:S(2)}, u32[]{:S(2)}) %collective-permute-start.3) | collective-permute-done | bytes 101408 | tf_op jit(solution)/shard_map/ppermute | solution.py:21
  33.6 12.3 %fusion.109 = (f32[16,24]{1,0:T(8,128)S(1)}, f32[16,24,768]{2,1,0:T(8,128)S(1)}) fusion(f32[768]{0:T(1024)S(1)} %get-tuple-element.49, f32[22,30,768]{2,1,0:T(8,128)S(1)} %maximum_convert_fusion, f32[768]{0:T(1024)S(1)} %get-tuple-element.50, f32[768]{0:T(1024)S(1)} %get-tuple-element.3, f32[768]{0:T(1024)S(1)} %get-tuple-element.4, ...), kind=kLoop, calls=%fused_computation.218 | loop fusion | flops 28900992 | bytes 59134464 | tf_op jit(solution)/shard_map/reduce_sum | solution.py:41
  46.8 57.7 %all-gather.5.cloned.1.call-done = bf16[768,3072]{1,0:T(8,128)(2,1)} async-done(((bf16[768,768]{1,0:T(8,128)(2,1)}), bf16[768,3072]{1,0:T(8,128)(2,1)}) %all-gather.5.cloned.1.call-update) | async-done | bytes 4718608 | tf_op jit(solution)/shard_map/all_gather | solution.py:63
  104.6 89.4 %all-gather.7.cloned.1.call-done = bf16[3072,768]{1,0:T(8,128)(2,1)} async-done(((bf16[768,768]{1,0:T(8,128)(2,1)}), bf16[3072,768]{1,0:T(8,128)(2,1)}) %all-gather.7.cloned.1.call-update) | async-done | bytes 4718608 | tf_op jit(solution)/shard_map/all_gather | solution.py:68
  193.9 7.9 %fusion.34 = bf16[384,768]{1,0:T(8,128)(2,1)S(1)} fusion(bf16[3072,768]{1,0:T(8,128)(2,1)} %all-gather.7.cloned.1.call-done, bf16[384,768]{1,0:T(8,128)(2,1)S(1)} %bitcast.66, bf16[384,768]{1,0:T(8,128)(2,1)S(1)} %bitcast.70, bf16[768,3072]{1,0:T(8,128)(2,1)} %all-gather.5.cloned.1.call-done), kind=kOutput, calls=%fused_computation.37 | convolution fusion | flops 3635380224 | bytes 11206656 | tf_op jit(solution)/shard_map/dot_general | solution.py:67
  201.9 42.4 %all-gather.9.cloned.1.call-done = bf16[768,1536]{1,0:T(8,128)(2,1)} async-done(((bf16[768,384]{1,0:T(8,128)(2,1)}), bf16[768,1536]{1,0:T(8,128)(2,1)}) %all-gather.9.cloned.1.call-update) | async-done | bytes 2359312 | tf_op jit(solution)/shard_map/all_gather | solution.py:74
  244.2 2.7 convolution_convert_fusion
  250.8 2.3 bitcast_reduce_fusion.1
  253.0 2.3 bitcast_reduce_fusion.2
  255.4 2.1 copy.22
  257.5 3.6 fusion.37
  261.1 3.0 fusion.11
  267.6 39.0 %pmax.7 = f32[512,12]{0,1:T(8,128)S(1)} all-reduce(f32[512,12]{0,1:T(8,128)S(1)} %pad_maximum_fusion), channel_id=1, replica_groups=mesh['row'=8,'col'=4] {'row','col'}, use_global_device_ids=true, to_apply=%region_5.0 | all-reduce | flops 6144 | bytes 49152 | tf_op jit(solution)/shard_map/pmax | solution.py:109
  307.3 2.7 maximum_multiply_fusion
  310.6 34.6 %reduce-scatter.3.cloned.1.call-done = f32[128,768]{0,1:T(8,128)} async-done(((f32[512,768]{0,1:T(8,128)}), f32[128,768]{0,1:T(8,128)}) %reduce-scatter.3.cloned.1.call-update) | async-done | bytes 393232 | tf_op jit(solution)/shard_map/reduce_scatter | solution.py:115
  346.0 19.4 %reduce-scatter.5.cloned.1.call-done = f32[128,12]{0,1:T(8,128)} async-done(((f32[512,12]{0,1:T(8,128)}), f32[128,12]{0,1:T(8,128)}) %reduce-scatter.5.cloned.1.call-update) | async-done | bytes 6160 | tf_op jit(solution)/shard_map/reduce_scatter | solution.py:114
  365.4 12.2 %psum.15 = f32[128,12]{0,1:T(8,128)S(1)} all-reduce(f32[128,12]{0,1:T(8,128)} %reduce-scatter.5.cloned.1.call-done), channel_id=1, replica_groups=mesh['row'=8,'col'=4] {'row'}, use_global_device_ids=true, to_apply=%region_12.0 | all-reduce | flops 1536 | bytes 12288 | tf_op jit(solution)/shard_map/psum | solution.py:117
  377.7 43.2 %all-reduce.2.cloned.1.call-done = f32[128,768]{0,1:T(8,128)} async-done(((f32[128,768]{0,1:T(8,128)}), f32[128,768]{0,1:T(8,128)}) %all-reduce.2.cloned.1.call-update) | async-done | bytes 393232 | tf_op jit(solution)/shard_map/psum | solution.py:117
  422.0 30.1 %all-gather.11.cloned.1.call-done = bf16[768,768]{0,1:T(8,128)(2,1)} async-done(((bf16[768,192]{0,1:T(8,128)(2,1)}), bf16[768,768]{0,1:T(8,128)(2,1)}) %all-gather.11.cloned.1.call-update) | async-done | bytes 1179664 | tf_op jit(solution)/shard_map/all_gather | solution.py:77
  454.0 17.9 %all_gather.19 = bf16[512,768]{1,0:T(8,128)(2,1)S(1)} all-gather(bf16[128,768]{1,0:T(8,128)(2,1)S(1)} %convolution_convert_fusion.1), channel_id=1, replica_groups=mesh['row'=8,'col'=4] {'col'}, dimensions={0}, use_global_device_ids=true | all-gather | bytes 983040 | tf_op jit(solution)/shard_map/all_gather | solution.py:121
  (65 shorter events, 20.4 us)
Async XLA Ops:
  7.2 1.6 copy-start.1
  7.2 97.4 %all-gather.5.cloned.1.call-start = ((), (), s32[]{:S(2)}) async-start(), calls=%async_computation.2 | async-start | bytes 5898240 | tf_op jit(solution)/shard_map/all_gather | solution.py:63
  7.9 4.6 copy-start.6
  7.9 4.8 %copy-start.2 = (bf16[512,768]{1,0:T(8,128)(2,1)S(1)}, bf16[512,768]{1,0:T(8,128)(2,1)}, u32[]{:S(2)}) copy-start(bf16[512,768]{1,0:T(8,128)(2,1)} %param.17) | copy-start | bytes 2359300
  7.9 186.0 %all-gather.7.cloned.1.call-start = ((), (), s32[]{:S(2)}) async-start(), calls=%async_computation.3 | async-start | bytes 5898240 | tf_op jit(solution)/shard_map/all_gather | solution.py:68
  8.7 235.6 %all-gather.9.cloned.1.call-start = ((), (), s32[]{:S(2)}) async-start(), calls=%async_computation.4 | async-start | bytes 2949120 | tf_op jit(solution)/shard_map/all_gather | solution.py:74
  8.8 5.3 %collective-permute-start = (bf16[3,24,768]{2,1,0:T(8,128)(2,1)S(1)}, bf16[3,24,768]{2,1,0:T(8,128)(2,1)S(1)}, u32[]{:S(2)}, u32[]{:S(2)}) collective-permute-start(bf16[3,24,768]{2,1,0:T(8,128)(2,1)S(1)} %get-tuple-element.62), channel_id=1, source_target_pairs={{0,4},{4,8},{8,12},{12,16},{16,20},{20,24},{24,28},{1,5},{5,9},{9,... | collective-permute-start | bytes 331784 | tf_op jit(solution)/shard_map/ppermute | solution.py:19
  11.2 5.3 %collective-permute-start.1 = (bf16[3,24,768]{2,1,0:T(8,128)(2,1)S(1)}, bf16[3,24,768]{2,1,0:T(8,128)(2,1)S(1)}, u32[]{:S(2)}, u32[]{:S(2)}) collective-permute-start(bf16[3,24,768]{2,1,0:T(8,128)(2,1)S(1)} %get-tuple-element.61), channel_id=1, source_target_pairs={{4,0},{8,4},{12,8},{16,12},{20,16},{24,20},{28,24},{5,1},{9,5},{13... | collective-permute-start | bytes 331784 | tf_op jit(solution)/shard_map/ppermute | solution.py:21
  12.5 332.7 %reduce-scatter.3.cloned.1.call-start = ((), (), s32[]{:S(2)}) async-start(), calls=%async_computation.5 | async-start | bytes 1966080 | tf_op jit(solution)/shard_map/reduce_scatter | solution.py:115
  16.6 9.2 %collective-permute-start.2 = (bf16[22,3,768]{2,1,0:T(4,128)(2,1)S(1)}, bf16[22,3,768]{2,1,0:T(4,128)(2,1)S(1)}, u32[]{:S(2)}, u32[]{:S(2)}) collective-permute-start(bf16[22,3,768]{2,1,0:T(4,128)(2,1)S(1)} %get-tuple-element.59), channel_id=1, source_target_pairs={{0,1},{1,2},{2,3},{4,5},{5,6},{6,7},{8,9},{9,10},{10,11},{12,13},{... | collective-permute-start | bytes 304136 | tf_op jit(solution)/shard_map/ppermute | solution.py:19
  20.1 13.1 %collective-permute-start.3 = (bf16[22,3,768]{2,1,0:T(4,128)(2,1)S(1)}, bf16[22,3,768]{2,1,0:T(4,128)(2,1)S(1)}, u32[]{:S(2)}, u32[]{:S(2)}) collective-permute-start(bf16[22,3,768]{2,1,0:T(4,128)(2,1)S(1)} %get-tuple-element.60), channel_id=1, source_target_pairs={{1,0},{2,1},{3,2},{5,4},{6,5},{7,6},{9,8},{10,9},{11,10},{13,12},{... | collective-permute-start | bytes 304136 | tf_op jit(solution)/shard_map/ppermute | solution.py:21
  45.9 0.7 copy-start.7
  45.9 0.7 copy-start.8
  201.9 45.1 %copy-start.10 = (bf16[384,768]{1,0:T(8,128)(2,1)}, bf16[384,768]{1,0:T(8,128)(2,1)S(1)}, u32[]{:S(2)}) copy-start(bf16[384,768]{1,0:T(8,128)(2,1)S(1)} %fusion.34) | copy-start | bytes 1769476
  248.9 1.8 copy-start.3
  248.9 1.8 copy-start.5
  257.5 3.6 copy-start
  261.1 3.0 copy-start.4
  310.0 142.2 %copy-start.9 = (f32[768]{0:T(1024)S(1)}, f32[768]{0:T(1024)}, u32[]{:S(2)}) copy-start(f32[768]{0:T(1024)} %param.18) | copy-start | bytes 9220
  310.0 55.4 %reduce-scatter.5.cloned.1.call-start = ((), (), s32[]{:S(2)}) async-start(), calls=%async_computation.7 | async-start | bytes 40960 | tf_op jit(solution)/shard_map/reduce_scatter | solution.py:114
  310.6 110.3 %all-reduce.2.cloned.1.call-start = ((), (), s32[]{:S(2)}) async-start(), calls=%async_computation.6 | async-start | bytes 786432 | tf_op jit(solution)/shard_map/psum | solution.py:117
  345.2 106.9 %all-gather.11.cloned.1.call-start = ((), (), s32[]{:S(2)}) async-start(), calls=%async_computation.8 | async-start | bytes 1474560 | tf_op jit(solution)/shard_map/all_gather | solution.py:77
Sparse Core Ops, SparseCore 0:
  9.6 94.9 all-gather.4
  106.1 87.7 all-gather.6
  195.6 48.6 all-gather.8
  310.1 35.0 reduce-scatter.2
  347.3 18.0 reduce-scatter.4
  368.4 52.5 all-reduce.1
  422.5 29.6 all-gather.10
where the time goes:
time: 480 us
  waiting for transfers between devices  334 us (70%)
  blocking collectives  69.1 us (14%)
  matrix products  25.5 us (5%)
  other arithmetic  21.2 us (4%)
  between operations  14.4 us (3%)
  starting transfers between devices  8.75 us (2%)
  local copies, waits for them, and re-layouts  7.14 us (1%)
    all_gather x1, waiting for transfers between devices, body(): lax.all_gather(w_out, 'col', axis=0, tiled=True)  89.4 us
    all_gather x1, waiting for transfers between devices, body(): lax.all_gather(w_in, 'col', axis=1, tiled=True)  57.7 us
    psum x1, waiting for transfers between devices, body(): den_share, num_share = lax.psum((den_part, num_part), 'row')  43.2 us
    all_gather x1, waiting for transfers between devices, body(): lax.all_gather(w_kv, 'col', axis=1, tiled=True)  42.4 us
    pmax x1, blocking collectives, body(): peak = lax.pmax(maxima, ('row', 'col'))  39 us
    reduce_scatter x1, waiting for transfers between devices, body(): lax.psum_scatter(num_terms, 'col', scatter_dimension=0, tiled=True)  34.6 us
    all_gather x1, waiting for transfers between devices, body(): w_full = lax.all_gather(w_o, 'col', axis=1, tiled=True)  30.1 us
    reduce_scatter x1, waiting for transfers between devices, body(): lax.psum_scatter(den_terms, 'col', scatter_dimension=0, tiled=True)  19.4 us
  transfers between devices with their start and end apart: 11, of which 10 were waited for; matrix products, arithmetic and copies ran while one was open for 5% of the time, Pallas kernels for 0%

commit v1 on v0

--- a/solution.py
+++ b/solution.py
@@ -74,7 +74,14 @@
         lax.all_gather(w_kv, "col", axis=1, tiled=True),
         preferred_element_type=jnp.float32,
     ).astype(jnp.bfloat16)
-    w_full = lax.all_gather(w_o, "col", axis=1, tiled=True)
+    size = lax.axis_size("col")
+    forward = [(i_2, (i_2 + 1) % size) for i_2 in range(size)]
+    blocks = [w_o]
+    for far in range(1, size):
+        blocks = [lax.ppermute(blocks[0], "col", forward), *blocks]
+    out = jnp.concatenate(blocks, axis=1)
+    turn = (lax.axis_index("col") + 1) * blocks[-1].shape[1]
+    w_full = jnp.roll(out, turn, axis=1)
     key_heads = keys_vals[:, :width_d].reshape(-1, HEADS, HEAD)
     val_heads = keys_vals[:, width_d:].reshape(-1, HEADS, HEAD)
     query_heads = queries.reshape(latent_count, HEADS, HEAD)

time: 480 us -> 465 us (0.969)
  waiting for transfers between devices: 334 us -> 309 us
  starting transfers between devices: 8.75 us -> 16.8 us
    ppermute x0 -> x3, waiting for transfers between devices: none -> 39.2 us  [body(): blocks = [lax.ppermute(blocks[0], 'col', forward), *blocks]]
    reduce_scatter x1, waiting for transfers between devices: 34.6 us -> 1.24 us  [body(): lax.psum_scatter(num_terms, 'col', scatter_dimension=0, tiled=True)]
    all_gather x1 -> x0, waiting for transfers between devices: 30.1 us -> none  [body(): w_full = lax.all_gather(w_o, 'col', axis=1, tiled=True)]
    ppermute x0 -> x3, starting transfers between devices: none -> 8.11 us  [body(): blocks = [lax.ppermute(blocks[0], 'col', forward), *blocks]]
  transfers between devices with their start and end apart: 11 -> 13, of which waited for: 10 -> 12; matrix products, arithmetic and copies ran while one was open for 5% -> 5% of each run, Pallas kernels for 0% -> 0%
where the time goes in v1:
time: 465 us
  waiting for transfers between devices  309 us (66%)
  blocking collectives  70.7 us (15%)
  matrix products  24.2 us (5%)
  other arithmetic  21.2 us (5%)
  starting transfers between devices  16.8 us (4%)
  between operations  14.5 us (3%)
  local copies, waits for them, and re-layouts  8.2 us (2%)
    all_gather x1, waiting for transfers between devices, body(): lax.all_gather(w_out, 'col', axis=0, tiled=True)  89.4 us
    all_gather x1, waiting for transfers between devices, body(): lax.all_gather(w_in, 'col', axis=1, tiled=True)  57.7 us
    psum x1, waiting for transfers between devices, body(): den_share, num_share = lax.psum((den_part, num_part), 'row')  43.3 us
    all_gather x1, waiting for transfers between devices, body(): lax.all_gather(w_kv, 'col', axis=1, tiled=True)  42.4 us
    ppermute x3, waiting for transfers between devices, body(): blocks = [lax.ppermute(blocks[0], 'col', forward), *blocks]  39.2 us
    pmax x1, blocking collectives, body(): peak = lax.pmax(maxima, ('row', 'col'))  39 us
    reduce_scatter x1, waiting for transfers between devices, body(): lax.psum_scatter(den_terms, 'col', scatter_dimension=0, tiled=True)  20.4 us
    all_gather x1, blocking collectives, body(): latents = lax.all_gather(own_rows, 'col', axis=0, tiled=True)  19.5 us
  transfers between devices with their start and end apart: 13, of which 12 were waited for; matrix products, arithmetic and copies ran while one was open for 5% of the time, Pallas kernels for 0%

profile of v1, /device:TPU:0, one launch (start us, length us, event | category | flops | bytes accessed | tf_op | source)
XLA Modules:
  0.0 464.7 jit_solution(15265887340997864318)
XLA Ops:
  8.8 2.4 collective-permute-start
  14.1 2.3 collective-permute-done.1
  16.6 3.5 collective-permute-start.2
  21.5 4.3 collective-permute-done.2
  25.8 7.4 %collective-permute-done.3 = bf16[22,3,768]{2,1,0:T(4,128)(2,1)S(1)} collective-permute-done((bf16[22,3,768]{2,1,0:T(4,128)(2,1)S(1)}, bf16[22,3,768]{2,1,0:T(4,128)(2,1)S(1)}, u32[]{:S(2)}, u32[]{:S(2)}) %collective-permute-start.3) | collective-permute-done | bytes 101408 | tf_op jit(solution)/shard_map/ppermute | solution.py:21
  33.6 12.3 %fusion.115 = (f32[16,24]{1,0:T(8,128)S(1)}, f32[16,24,768]{2,1,0:T(8,128)S(1)}) fusion(f32[768]{0:T(1024)S(1)} %get-tuple-element.49, f32[22,30,768]{2,1,0:T(8,128)S(1)} %maximum_convert_fusion, f32[768]{0:T(1024)S(1)} %get-tuple-element.50, f32[768]{0:T(1024)S(1)} %get-tuple-element.3, f32[768]{0:T(1024)S(1)} %get-tuple-element.4, ...), kind=kLoop, calls=%fused_computation.229 | loop fusion | flops 28900992 | bytes 59134464 | tf_op jit(solution)/shard_map/reduce_sum | solution.py:41
  46.8 57.7 %all-gather.4.cloned.1.call-done = bf16[768,3072]{1,0:T(8,128)(2,1)} async-done(((bf16[768,768]{1,0:T(8,128)(2,1)}), bf16[768,3072]{1,0:T(8,128)(2,1)}) %all-gather.4.cloned.1.call-update) | async-done | bytes 4718608 | tf_op jit(solution)/shard_map/all_gather | solution.py:63
  104.6 89.4 %all-gather.6.cloned.1.call-done = bf16[3072,768]{1,0:T(8,128)(2,1)} async-done(((bf16[768,768]{1,0:T(8,128)(2,1)}), bf16[3072,768]{1,0:T(8,128)(2,1)}) %all-gather.6.cloned.1.call-update) | async-done | bytes 4718608 | tf_op jit(solution)/shard_map/all_gather | solution.py:68
  193.9 7.9 %fusion.34 = bf16[384,768]{1,0:T(8,128)(2,1)S(1)} fusion(bf16[3072,768]{1,0:T(8,128)(2,1)} %all-gather.6.cloned.1.call-done, bf16[384,768]{1,0:T(8,128)(2,1)S(1)} %bitcast.65, bf16[384,768]{1,0:T(8,128)(2,1)S(1)} %bitcast.69, bf16[768,3072]{1,0:T(8,128)(2,1)} %all-gather.4.cloned.1.call-done), kind=kOutput, calls=%fused_computation.37 | convolution fusion | flops 3635380224 | bytes 11206656 | tf_op jit(solution)/shard_map/dot_general | solution.py:67
  201.9 42.4 %all-gather.8.cloned.1.call-done = bf16[768,1536]{1,0:T(8,128)(2,1)} async-done(((bf16[768,384]{1,0:T(8,128)(2,1)}), bf16[768,1536]{1,0:T(8,128)(2,1)}) %all-gather.8.cloned.1.call-update) | async-done | bytes 2359312 | tf_op jit(solution)/shard_map/all_gather | solution.py:74
  244.2 2.7 convolution_convert_fusion
  257.5 3.6 fusion.37
  261.1 3.0 fusion.11
  267.6 39.0 %pmax.7 = f32[512,12]{0,1:T(8,128)S(1)} all-reduce(f32[512,12]{0,1:T(8,128)S(1)} %pad_maximum_fusion), channel_id=1, replica_groups=mesh['row'=8,'col'=4] {'row','col'}, use_global_device_ids=true, to_apply=%region_5.6 | all-reduce | flops 6144 | bytes 49152 | tf_op jit(solution)/shard_map/pmax | solution.py:116
  307.3 2.7 maximum_multiply_fusion
  312.6 10.9 %collective-permute-done.4 = bf16[768,192]{0,1:T(8,128)(2,1)S(1)} collective-permute-done((bf16[768,192]{0,1:T(8,128)(2,1)S(1)}, bf16[768,192]{0,1:T(8,128)(2,1)S(1)}, u32[]{:S(2)}, u32[]{:S(2)}) %collective-permute-start.4) | collective-permute-done | bytes 294944 | tf_op jit(solution)/shard_map/ppermute | solution.py:81
  323.5 2.5 collective-permute-start.5
  325.9 13.8 %collective-permute-done.5 = bf16[768,192]{0,1:T(8,128)(2,1)S(1)} collective-permute-done((bf16[768,192]{0,1:T(8,128)(2,1)S(1)}, bf16[768,192]{0,1:T(8,128)(2,1)S(1)}, u32[]{:S(2)}, u32[]{:S(2)}) %collective-permute-start.5) | collective-permute-done | bytes 294944 | tf_op jit(solution)/shard_map/ppermute | solution.py:81
  339.7 4.0 collective-permute-start.6
  343.7 14.6 %collective-permute-done.6 = bf16[768,192]{0,1:T(8,128)(2,1)S(1)} collective-permute-done((bf16[768,192]{0,1:T(8,128)(2,1)S(1)}, bf16[768,192]{0,1:T(8,128)(2,1)S(1)}, u32[]{:S(2)}, u32[]{:S(2)}) %collective-permute-start.6) | collective-permute-done | bytes 294944 | tf_op jit(solution)/shard_map/ppermute | solution.py:81
  359.8 20.4 %reduce-scatter.5.cloned.1.call-done = f32[128,12]{0,1:T(8,128)} async-done(((f32[512,12]{0,1:T(8,128)}), f32[128,12]{0,1:T(8,128)}) %reduce-scatter.5.cloned.1.call-update) | async-done | bytes 6160 | tf_op jit(solution)/shard_map/reduce_scatter | solution.py:121
  380.2 12.2 %psum.15 = f32[128,12]{0,1:T(8,128)S(1)} all-reduce(f32[128,12]{0,1:T(8,128)} %reduce-scatter.5.cloned.1.call-done), channel_id=1, replica_groups=mesh['row'=8,'col'=4] {'row'}, use_global_device_ids=true, to_apply=%region_12.13 | all-reduce | flops 1536 | bytes 12288 | tf_op jit(solution)/shard_map/psum | solution.py:124
  392.4 43.3 %all-reduce.2.cloned.1.call-done = f32[128,768]{0,1:T(8,128)} async-done(((f32[128,768]{0,1:T(8,128)}), f32[128,768]{0,1:T(8,128)}) %all-reduce.2.cloned.1.call-update) | async-done | bytes 393232 | tf_op jit(solution)/shard_map/psum | solution.py:124
  437.5 19.5 %all_gather.15 = bf16[512,768]{1,0:T(8,128)(2,1)S(1)} all-gather(bf16[128,768]{1,0:T(8,128)(2,1)S(1)} %fusion.96), channel_id=1, replica_groups=mesh['row'=8,'col'=4] {'col'}, dimensions={0}, use_global_device_ids=true | all-gather | bytes 983040 | tf_op jit(solution)/shard_map/all_gather | solution.py:128
  (78 shorter events, 28.5 us)
Async XLA Ops:
  7.2 1.6 copy-start.2
  7.2 97.4 %all-gather.4.cloned.1.call-start = ((), (), s32[]{:S(2)}) async-start(), calls=%async_computation.2 | async-start | bytes 5898240 | tf_op jit(solution)/shard_map/all_gather | solution.py:63
  7.9 4.6 copy-start.7
  7.9 4.8 %copy-start.3 = (bf16[512,768]{1,0:T(8,128)(2,1)S(1)}, bf16[512,768]{1,0:T(8,128)(2,1)}, u32[]{:S(2)}) copy-start(bf16[512,768]{1,0:T(8,128)(2,1)} %param.17) | copy-start | bytes 2359300
  7.9 186.0 %all-gather.6.cloned.1.call-start = ((), (), s32[]{:S(2)}) async-start(), calls=%async_computation.3 | async-start | bytes 5898240 | tf_op jit(solution)/shard_map/all_gather | solution.py:68
  8.7 235.6 %all-gather.8.cloned.1.call-start = ((), (), s32[]{:S(2)}) async-start(), calls=%async_computation.4 | async-start | bytes 2949120 | tf_op jit(solution)/shard_map/all_gather | solution.py:74
  8.8 5.3 %collective-permute-start = (bf16[3,24,768]{2,1,0:T(8,128)(2,1)S(1)}, bf16[3,24,768]{2,1,0:T(8,128)(2,1)S(1)}, u32[]{:S(2)}, u32[]{:S(2)}) collective-permute-start(bf16[3,24,768]{2,1,0:T(8,128)(2,1)S(1)} %get-tuple-element.62), channel_id=1, source_target_pairs={{0,4},{4,8},{8,12},{12,16},{16,20},{20,24},{24,28},{1,5},{5,9},{9,... | collective-permute-start | bytes 331784 | tf_op jit(solution)/shard_map/ppermute | solution.py:19
  11.2 5.3 %collective-permute-start.1 = (bf16[3,24,768]{2,1,0:T(8,128)(2,1)S(1)}, bf16[3,24,768]{2,1,0:T(8,128)(2,1)S(1)}, u32[]{:S(2)}, u32[]{:S(2)}) collective-permute-start(bf16[3,24,768]{2,1,0:T(8,128)(2,1)S(1)} %get-tuple-element.61), channel_id=1, source_target_pairs={{4,0},{8,4},{12,8},{16,12},{20,16},{24,20},{28,24},{5,1},{9,5},{13... | collective-permute-start | bytes 331784 | tf_op jit(solution)/shard_map/ppermute | solution.py:21
  12.5 347.2 %reduce-scatter.3.cloned.1.call-start = ((), (), s32[]{:S(2)}) async-start(), calls=%async_computation.5 | async-start | bytes 1966080 | tf_op jit(solution)/shard_map/reduce_scatter | solution.py:122
  16.6 9.2 %collective-permute-start.2 = (bf16[22,3,768]{2,1,0:T(4,128)(2,1)S(1)}, bf16[22,3,768]{2,1,0:T(4,128)(2,1)S(1)}, u32[]{:S(2)}, u32[]{:S(2)}) collective-permute-start(bf16[22,3,768]{2,1,0:T(4,128)(2,1)S(1)} %get-tuple-element.59), channel_id=1, source_target_pairs={{0,1},{1,2},{2,3},{4,5},{5,6},{6,7},{8,9},{9,10},{10,11},{12,13},{... | collective-permute-start | bytes 304136 | tf_op jit(solution)/shard_map/ppermute | solution.py:19
  20.1 13.1 %collective-permute-start.3 = (bf16[22,3,768]{2,1,0:T(4,128)(2,1)S(1)}, bf16[22,3,768]{2,1,0:T(4,128)(2,1)S(1)}, u32[]{:S(2)}, u32[]{:S(2)}) collective-permute-start(bf16[22,3,768]{2,1,0:T(4,128)(2,1)S(1)} %get-tuple-element.60), channel_id=1, source_target_pairs={{1,0},{2,1},{3,2},{5,4},{6,5},{7,6},{9,8},{10,9},{11,10},{13,12},{... | collective-permute-start | bytes 304136 | tf_op jit(solution)/shard_map/ppermute | solution.py:21
  45.9 0.7 copy-start.9
  201.9 45.1 %copy-start.11 = (bf16[384,768]{1,0:T(8,128)(2,1)}, bf16[384,768]{1,0:T(8,128)(2,1)S(1)}, u32[]{:S(2)}) copy-start(bf16[384,768]{1,0:T(8,128)(2,1)S(1)} %fusion.34) | copy-start | bytes 1769476
  248.9 1.8 copy-start.4
  248.9 1.8 copy-start.6
  257.5 3.6 copy-start
  261.1 3.0 copy-start.5
  310.0 1.0 copy-start.1
  310.0 70.2 %reduce-scatter.5.cloned.1.call-start = ((), (), s32[]{:S(2)}) async-start(), calls=%async_computation.7 | async-start | bytes 40960 | tf_op jit(solution)/shard_map/reduce_scatter | solution.py:121
  310.9 12.5 %collective-permute-start.4 = (bf16[768,192]{0,1:T(8,128)(2,1)S(1)}, bf16[768,192]{0,1:T(8,128)(2,1)S(1)}, u32[]{:S(2)}, u32[]{:S(2)}) collective-permute-start(bf16[768,192]{0,1:T(8,128)(2,1)S(1)} %copy-done.1), channel_id=1, source_target_pairs={{0,1},{1,2},{2,3},{3,0},{4,5},{5,6},{6,7},{7,4},{8,9},{9,10},{10,1... | collective-permute-start | bytes 884744 | tf_op jit(solution)/shard_map/ppermute | solution.py:81
  323.5 16.2 %collective-permute-start.5 = (bf16[768,192]{0,1:T(8,128)(2,1)S(1)}, bf16[768,192]{0,1:T(8,128)(2,1)S(1)}, u32[]{:S(2)}, u32[]{:S(2)}) collective-permute-start(bf16[768,192]{0,1:T(8,128)(2,1)S(1)} %collective-permute-done.4), channel_id=1, source_target_pairs={{0,1},{1,2},{2,3},{3,0},{4,5},{5,6},{6,7},{7,4},{8,9},{9,10},{10,1... | collective-permute-start | bytes 884744 | tf_op jit(solution)/shard_map/ppermute | solution.py:81
  339.7 18.5 %collective-permute-start.6 = (bf16[768,192]{0,1:T(8,128)(2,1)S(1)}, bf16[768,192]{0,1:T(8,128)(2,1)S(1)}, u32[]{:S(2)}, u32[]{:S(2)}) collective-permute-start(bf16[768,192]{0,1:T(8,128)(2,1)S(1)} %collective-permute-done.5), channel_id=1, source_target_pairs={{0,1},{1,2},{2,3},{3,0},{4,5},{5,6},{6,7},{7,4},{8,9},{9,10},{10,1... | collective-permute-start | bytes 884744 | tf_op jit(solution)/shard_map/ppermute | solution.py:81
  358.4 77.3 %all-reduce.2.cloned.1.call-start = ((), (), s32[]{:S(2)}) async-start(), calls=%async_computation.6 | async-start | bytes 786432 | tf_op jit(solution)/shard_map/psum | solution.py:124
  359.7 77.1 %copy-start.10 = (f32[768]{0:T(1024)S(1)}, f32[768]{0:T(1024)}, u32[]{:S(2)}) copy-start(f32[768]{0:T(1024)} %param.18) | copy-start | bytes 9220
  (1 other events, 0.7 us)
Sparse Core Ops, SparseCore 0:
  9.6 94.9 all-gather.3
  106.1 87.7 all-gather.5
  195.6 48.6 all-gather.7
  310.1 49.5 reduce-scatter.2
  361.8 18.3 reduce-scatter.4
  383.1 52.5 all-reduce.1
